TPU v7x, 32 devices: a whole 2x2x4 slice. The times are simulated.
32 devices in a mesh: row: 8 (over z, y), col: 4 (over x, core).
Axes of the slice: x: 2, y: 2, z: 4, core: 2. Of those that a mesh axis runs over, the one named last changes fastest.
Arguments:
- head_deflections: float32 [256, 3, 2, 1024], P('row', None, None, 'col'), may hold values from -6 to 6
- diag_inverse: float32 [2, 1024, 1024], P(None, None, 'col'), may hold values from -1 to 2, as said below
- coupling: float32 [1024, 1024], P(None, 'col'), may hold values from -0.1875 to 0.1875
- panel_factor: float32 [8192, 2, 1024], P('row', None, 'col'), may hold values from -0.125 to 0.125
- trailing: float32 [256, 3, 8192], P('col', None, 'row'), may hold values from -6 to 6
Outputs:
- solved: float32 [256, 3, 2, 1024], P('row', None, None, 'col')
- rest: float32 [256, 3, 8192], P('col', None, 'row')
Inputs may be any that keep to these rules, and one draw needn't show every extreme that they name: Each diag_inverse[p] is lower triangular with a positive diagonal.
All inputs are finite; a program needn't handle non-finite values.
Results may differ from a plain program's by a relative error of at most 0.00007.
Values sent between devices are 32-bit elements; how exact they have to be, the bound alone decides.
No kernel may reach another device: no remote copies, remote signals or barrier semaphores. Data moves between devices by JAX's collectives and lax.ppermute only.
A program may use at most 64 MiB of HBM per device.

v0:
```python
import jax
import jax.numpy as jnp
from jax import lax
from jax.sharding import PartitionSpec as P


def apply_cols(matrix, vectors):
    return lax.dot_general(
        vectors,
        matrix,
        (((2,), (1,)), ((), ())),
        precision=lax.Precision.HIGHEST,
        preferred_element_type=jnp.float32,
    )


def solve_first(block_rhs, diag_inverse):
    return lax.psum_scatter(
        apply_cols(diag_inverse[0], block_rhs), "col", scatter_dimension=2, tiled=True
    )


def solve_second(block_rhs, first_solved, diag_inverse, coupling):
    moved = lax.psum_scatter(
        apply_cols(coupling, first_solved), "col", scatter_dimension=2, tiled=True
    )
    carried = block_rhs - moved
    return lax.psum_scatter(
        apply_cols(diag_inverse[1], carried), "col", scatter_dimension=2, tiled=True
    )


def share_steps(solved_own):
    return lax.all_gather(solved_own, "row", axis=0, tiled=True)


def panel_terms(solved_all, factor):
    return lax.dot_general(
        solved_all,
        factor,
        (((2,), (1,)), ((), ())),
        precision=lax.Precision.HIGHEST,
        preferred_element_type=jnp.float32,
    )


def both_terms(first_all, second_all, panel_factor):
    first_part = panel_terms(first_all, panel_factor[:, 0, :])
    return first_part + panel_terms(second_all, panel_factor[:, 1, :])


def body(head_deflections, diag_inverse, coupling, panel_factor, trailing):
    first_own = solve_first(head_deflections[:, :, 0, :], diag_inverse)
    first_all = share_steps(first_own)
    second_own = solve_second(head_deflections[:, :, 1, :], first_own, diag_inverse, coupling)
    second_all = share_steps(second_own)
    summed = lax.psum_scatter(
        both_terms(first_all, second_all, panel_factor), "col", scatter_dimension=0, tiled=True
    )
    rest = trailing - summed
    solved = jnp.stack([first_own, second_own], axis=2)
    return (solved, rest)


def solution(mesh):
    placed = (
        P("row", None, None, "col"),
        P(None, None, "col"),
        P(None, "col"),
        P("row", None, "col"),
        P("col", None, "row"),
    )
    return jax.shard_map(
        body,
        mesh=mesh,
        in_specs=placed,
        out_specs=(P("row", None, None, "col"), P("col", None, "row")),
        check_vma=False,
    )
```

profile of v0, /device:TPU:0, one launch (start us, length us, event | category | flops | bytes accessed | tf_op | source)
XLA Modules:
  0.0 187.3 jit_solution(2642508243679747117)
XLA Ops:
  7.2 0.0 copy-start
  7.2 0.0 copy-start.1
  7.2 0.0 reduce-scatter.5.cloned.1.call-start
  7.2 1.3 fusion.12
  8.6 3.1 %fusion.5 = f32[32,3,1024]{2,0,1:T(8,128)} fusion(f32[2,1024,256]{2,1,0:T(8,128)} %param.6, f32[32,3,1,256]{3,2,1,0:T(1,128)S(1)} %get-tuple-element.9), kind=kOutput, calls=%fused_computation.8 | convolution fusion | flops 301989888 | bytes 1540096 | tf_op jit(solution)/shard_map/dot_general | solution.py:8
  11.7 0.0 reduce-scatter.5.cloned.1.call-update
  11.7 0.0 reduce-scatter.7.cloned.1.call-start
  11.8 23.7 %reduce-scatter.5.cloned.1.call-done = f32[32,3,256]{2,0,1:T(8,128)} async-done(((f32[32,3,1024]{2,0,1:T(8,128)}), f32[32,3,256]{2,0,1:T(8,128)}) %reduce-scatter.5.cloned.1.call-update) | async-done | bytes 98320 | tf_op jit(solution)/shard_map/reduce_scatter | solution.py:18
  35.4 0.0 copy-done
  35.4 2.8 %fusion.3 = f32[32,3,1024]{2,0,1:T(8,128)} fusion(f32[32,3,256]{2,0,1:T(8,128)} %reduce-scatter.5.cloned.1.call-done, f32[1024,256]{1,0:T(8,128)S(1)} %copy-done), kind=kOutput, calls=%fused_computation.6 | convolution fusion | flops 301989888 | bytes 1540096 | tf_op jit(solution)/shard_map/dot_general | solution.py:8
  38.2 0.0 reduce-scatter.7.cloned.1.call-update
  38.2 0.0 reduce-scatter.9.cloned.1.call-start
  38.3 21.1 %reduce-scatter.7.cloned.1.call-done = f32[32,3,256]{2,0,1:T(8,128)} async-done(((f32[32,3,1024]{2,0,1:T(8,128)}), f32[32,3,256]{2,0,1:T(8,128)}) %reduce-scatter.7.cloned.1.call-update) | async-done | bytes 98320 | tf_op jit(solution)/shard_map/reduce_scatter | solution.py:24
  59.3 0.0 copy-done.1
  59.3 2.8 %fusion.1 = f32[32,3,1024]{2,0,1:T(8,128)} fusion(f32[2,1024,256]{2,1,0:T(8,128)S(1)} %copy-done.1, f32[32,3,256]{2,0,1:T(8,128)} %reduce-scatter.7.cloned.1.call-done, f32[32,3,1,256]{3,2,1,0:T(1,128)S(1)} %get-tuple-element.8), kind=kOutput, calls=%fused_computation.4 | convolution fusion | flops 302014464 | bytes 1638400 | tf_op jit(solution)/shard_map/dot_general | solution.py:8
  62.1 0.0 reduce-scatter.9.cloned.1.call-update
  62.1 0.0 copy-start.2
  62.2 0.0 reduce-scatter.11.cloned.1.call-start
  62.2 4.0 %fusion.11 = (f32[1024,1,256]{2,1,0:T(1,128)S(1)}, f32[1024,1,256]{2,1,0:T(1,128)S(1)}) fusion(f32[1024,2,256]{2,1,0:T(2,128)} %param.8), kind=kLoop, calls=%fused_computation.16 | loop fusion | bytes 4194304 | tf_op jit(solution)/shard_map/slice | solution.py:49
  66.2 0.0 copy-done.2
  66.2 32.2 %all_gather.6 = f32[256,3,256]{2,0,1:T(8,128)S(1)} all-gather(f32[32,3,256]{2,0,1:T(8,128)S(1)} %copy-done.2), channel_id=1, replica_groups=mesh['row'=8,'col'=4] {'row'}, dimensions={0}, use_global_device_ids=true | all-gather | bytes 884736 | tf_op jit(solution)/shard_map/all_gather | solution.py:34
  98.4 4.3 %fusion = f32[256,3,1024]{2,0,1:T(8,128)} fusion(f32[256,3,256]{2,0,1:T(8,128)S(1)} %all_gather.6, f32[1024,1,256]{2,1,0:T(1,128)S(1)} %get-tuple-element.7), kind=kOutput, calls=%fused_computation.3 | convolution fusion | flops 2415919104 | bytes 4980736 | tf_op jit(solution)/shard_map/dot_general | solution.py:38
  102.7 0.0 reduce-scatter.9.cloned.1.call-done
  102.7 31.9 %all_gather.7 = f32[256,3,256]{2,0,1:T(8,128)S(1)} all-gather(f32[32,3,256]{2,0,1:T(8,128)} %reduce-scatter.9.cloned.1.call-done), channel_id=1, replica_groups=mesh['row'=8,'col'=4] {'row'}, dimensions={0}, use_global_device_ids=true | all-gather | bytes 884736 | tf_op jit(solution)/shard_map/all_gather | solution.py:34
  134.6 5.7 %convolution_add_fusion = f32[256,3,1024]{2,0,1:T(8,128)} fusion(f32[256,3,1024]{2,0,1:T(8,128)} %fusion, f32[256,3,256]{2,0,1:T(8,128)S(1)} %all_gather.7, f32[1024,1,256]{2,1,0:T(1,128)S(1)} %get-tuple-element.6), kind=kOutput, calls=%fused_computation | convolution fusion | flops 2416705536 | bytes 8126464 | tf_op jit(solution)/shard_map/dot_general | solution.py:38
  140.3 0.0 copy-start.4
  140.3 0.0 reduce-scatter.11.cloned.1.call-update
  140.3 0.9 copy-done.4
  141.2 0.8 copy.16
  142.0 36.6 %reduce-scatter.11.cloned.1.call-done = f32[64,3,1024]{2,0,1:T(8,128)} async-done(((f32[256,3,1024]{2,0,1:T(8,128)}), f32[64,3,1024]{2,0,1:T(8,128)}) %reduce-scatter.11.cloned.1.call-update) | async-done | bytes 786448 | tf_op jit(solution)/shard_map/reduce_scatter | solution.py:57
  178.6 0.0 copy-done.3
  178.6 2.1 %sub.7 = f32[64,3,1024]{2,0,1:T(8,128)} subtract(f32[64,3,1024]{2,0,1:T(8,128)S(1)} %copy-done.3, f32[64,3,1024]{2,0,1:T(8,128)} %reduce-scatter.11.cloned.1.call-done) | non-fusion elementwise | flops 196608 | bytes 2359296 | tf_op jit(solution)/shard_map/sub | solution.py:60
  (2 shorter events, 0.0 us)
Async XLA Ops:
  7.2 28.3 %copy-start = (f32[1024,256]{1,0:T(8,128)S(1)}, f32[1024,256]{1,0:T(8,128)}, u32[]{:S(2)}) copy-start(f32[1024,256]{1,0:T(8,128)} %param.7) | copy-start | bytes 3145732
  7.2 52.2 %copy-start.1 = (f32[2,1024,256]{2,1,0:T(8,128)S(1)}, f32[2,1024,256]{2,1,0:T(8,128)}, u32[]{:S(2)}) copy-start(f32[2,1024,256]{2,1,0:T(8,128)} %param.6) | copy-start | bytes 6291460
  7.2 28.2 %reduce-scatter.5.cloned.1.call-start = ((), (), s32[]{:S(2)}) async-start(), calls=%async_computation.4 | async-start | bytes 491520 | tf_op jit(solution)/shard_map/reduce_scatter | solution.py:18
  11.7 47.6 %reduce-scatter.7.cloned.1.call-start = ((), (), s32[]{:S(2)}) async-start(), calls=%async_computation.5 | async-start | bytes 491520 | tf_op jit(solution)/shard_map/reduce_scatter | solution.py:24
  38.2 64.5 %reduce-scatter.9.cloned.1.call-start = ((), (), s32[]{:S(2)}) async-start(), calls=%async_computation.6 | async-start | bytes 491520 | tf_op jit(solution)/shard_map/reduce_scatter | solution.py:28
  62.1 4.1 %copy-start.2 = (f32[32,3,256]{2,0,1:T(8,128)S(1)}, f32[32,3,256]{2,0,1:T(8,128)}, u32[]{:S(2)}) copy-start(f32[32,3,256]{2,0,1:T(8,128)} %reduce-scatter.5.cloned.1.call-done) | copy-start | bytes 294916
  62.2 116.5 %reduce-scatter.11.cloned.1.call-start = ((), (), s32[]{:S(2)}) async-start(), calls=%async_computation.7 | async-start | bytes 3932160 | tf_op jit(solution)/shard_map/reduce_scatter | solution.py:57
  140.3 0.9 copy-start.4
  140.3 38.4 %copy-start.3 = (f32[64,3,1024]{2,0,1:T(8,128)S(1)}, f32[64,3,1024]{2,0,1:T(8,128)}, u32[]{:S(2)}) copy-start(f32[64,3,1024]{2,0,1:T(8,128)} %param.9) | copy-start | bytes 2359300
Sparse Core Ops, SparseCore 0:
  11.8 23.5 reduce-scatter.4
  38.5 20.8 reduce-scatter.6
  62.4 20.8 reduce-scatter.8
  140.4 38.1 reduce-scatter.10
where the time goes:
time: 188 us; the launch traced here: 187 us
  waiting for transfers between devices  81.4 us (43%)
  blocking collectives  64 us (34%)
  matrix products  18.7 us (10%)
  between operations  13.8 us (7%)
  local copies, waits for them, and re-layouts  7.09 us (4%)
  other arithmetic  2.12 us (1%)
    all_gather x2, blocking collectives, share_steps(): return lax.all_gather(solved_own, 'row', axis=0, tiled=True)  64 us
    reduce_scatter x1, waiting for transfers between devices, body(): lax.psum_scatter(both_terms(first_all, second_all, panel_factor), 'col',...  36.6 us
    reduce_scatter x1, waiting for transfers between devices, solve_first(): lax.psum_scatter(apply_cols(diag_inverse[0], block_rhs), 'col', scatter_d...  23.7 us
    reduce_scatter x1, waiting for transfers between devices, solve_second(): lax.psum_scatter(apply_cols(coupling, first_solved), 'col', scatter_dimen...  21.1 us
    dot_general x2, matrix products, panel_terms(): lax.dot_general(solved_all, factor, (((2,), (1,)), ((), ())), precision=l...  10 us
    dot_general x3, matrix products, apply_cols(): lax.dot_general(vectors, matrix, (((2,), (1,)), ((), ())), precision=lax....  8.65 us
    slice x1, local copies, waits for them, and re-layouts, both_terms(): return first_part + panel_terms(second_all, panel_factor[:, 1, :])  4.02 us
  transfers between devices with their start and end apart: 4, of which 3 were waited for; matrix products, arithmetic and copies ran while one was open for 5% of the time, Pallas kernels for 0%

commit v1 on v0

--- a/solution.py
+++ b/solution.py
@@ -2,6 +2,18 @@
 import jax.numpy as jnp
 from jax import lax
 from jax.sharding import PartitionSpec as P
+
+
+def doubled_up(shard, axis, dim):
+    ways, here, step = (lax.axis_size(axis), lax.axis_index(axis), shard.shape[dim])
+    line, have = (shard, 1)
+    while have < ways:
+        line = jnp.concatenate(
+            [line, lax.ppermute(line, axis, [(d, (d - have) % ways) for d in range(ways)])],
+            axis=dim,
+        )
+        have = 2 * have
+    return jnp.roll(line, here * step, axis=dim)
 
 
 def apply_cols(matrix, vectors):
@@ -31,7 +43,7 @@
 
 
 def share_steps(solved_own):
-    return lax.all_gather(solved_own, "row", axis=0, tiled=True)
+    return doubled_up(solved_own, "row", 0)
 
 
 def panel_terms(solved_all, factor):

time: 188 us -> 190 us (1.011)
  blocking collectives: 64 us -> 0 us
  waiting for transfers between devices: 81.4 us -> 136 us
  starting transfers between devices: 0.16 us -> 8.75 us
  other arithmetic: 2.12 us -> 5.6 us
    all_gather x2 -> x0, blocking collectives: 64 us -> none  [share_steps(): return lax.all_gather(solved_own, 'row', axis=0, tiled=True)]
    ppermute x0 -> x6, waiting for transfers between devices: none -> 30.3 us  [doubled_up(): lax.ppermute(line, axis, [(d, (d - have) % ways) for d in range(ways)])]
    reduce_scatter x1, waiting for transfers between devices: 0.01 us -> 21.1 us  [solve_second(): lax.psum_scatter(apply_cols(diag_inverse[1], carried), 'col', scatter_dim...]
    ppermute x0 -> x6, starting transfers between devices: none -> 8.58 us  [doubled_up(): lax.ppermute(line, axis, [(d, (d - have) % ways) for d in range(ways)])]
    concatenate x0 -> x4, other arithmetic: none -> 3.48 us  [doubled_up(): jnp.concatenate([line, lax.ppermute(line, axis, [(d, (d - have) % ways) f...]
    reduce_scatter x1, waiting for transfers between devices: 36.6 us -> 40 us  [body(): lax.psum_scatter(both_terms(first_all, second_all, panel_factor), 'col',...]
  transfers between devices with their start and end apart: 4 -> 10, of which waited for: 3 -> 9; matrix products, arithmetic and copies ran while one was open for 5% -> 7% of each run, Pallas kernels for 0% -> 0%
where the time goes in v1:
time: 190 us; the launch traced here: 189 us
  waiting for transfers between devices  136 us (72%)
  matrix products  18.8 us (10%)
  between operations  13.8 us (7%)
  starting transfers between devices  8.75 us (5%)
  local copies, waits for them, and re-layouts  6.16 us (3%)
  other arithmetic  5.6 us (3%)
    reduce_scatter x1, waiting for transfers between devices, body(): lax.psum_scatter(both_terms(first_all, second_all, panel_factor), 'col',...  40 us
    ppermute x6, waiting for transfers between devices, doubled_up(): lax.ppermute(line, axis, [(d, (d - have) % ways) for d in range(ways)])  30.3 us
    reduce_scatter x1, waiting for transfers between devices, solve_first(): lax.psum_scatter(apply_cols(diag_inverse[0], block_rhs), 'col', scatter_d...  23.7 us
    reduce_scatter x1, waiting for transfers between devices, solve_second(): lax.psum_scatter(apply_cols(diag_inverse[1], carried), 'col', scatter_dim...  21.1 us
    reduce_scatter x1, waiting for transfers between devices, solve_second(): lax.psum_scatter(apply_cols(coupling, first_solved), 'col', scatter_dimen...  21.1 us
    dot_general x2, matrix products, panel_terms(): lax.dot_general(solved_all, factor, (((2,), (1,)), ((), ())), precision=l...  10.1 us
    dot_general x3, matrix products, apply_cols(): lax.dot_general(vectors, matrix, (((2,), (1,)), ((), ())), precision=lax....  8.79 us
    ppermute x6, starting transfers between devices, doubled_up(): lax.ppermute(line, axis, [(d, (d - have) % ways) for d in range(ways)])  8.58 us
  transfers between devices with their start and end apart: 10, of which 9 were waited for; matrix products, arithmetic and copies ran while one was open for 7% of the time, Pallas kernels for 0%

profile of v1, /device:TPU:0, one launch (start us, length us, event | category | flops | bytes accessed | tf_op | source)
XLA Modules:
  0.0 189.4 jit_solution(3946796657077684964)
XLA Ops:
  7.2 0.0 reduce-scatter.5.cloned.1.call-start
  7.2 1.3 fusion.34
  8.5 3.2 %fusion.5 = f32[32,3,1024]{2,0,1:T(8,128)} fusion(f32[2,1024,256]{2,1,0:T(8,128)} %param.8, f32[32,3,1,256]{3,2,1,0:T(1,128)S(1)} %get-tuple-element.10), kind=kOutput, calls=%fused_computation.24 | convolution fusion | flops 301989888 | bytes 1540096 | tf_op jit(solution)/shard_map/dot_general | solution.py:20
  11.8 0.0 reduce-scatter.5.cloned.1.call-update
  11.8 0.0 reduce-scatter.7.cloned.1.call-start
  11.8 23.7 %reduce-scatter.5.cloned.1.call-done = f32[32,3,256]{2,0,1:T(8,128)} async-done(((f32[32,3,1024]{2,0,1:T(8,128)}), f32[32,3,256]{2,0,1:T(8,128)}) %reduce-scatter.5.cloned.1.call-update) | async-done | bytes 98320 | tf_op jit(solution)/shard_map/reduce_scatter | solution.py:30
  35.5 2.8 %fusion.3 = f32[32,3,1024]{2,0,1:T(8,128)} fusion(f32[32,3,256]{2,0,1:T(8,128)} %reduce-scatter.5.cloned.1.call-done, f32[1024,256]{1,0:T(8,128)S(1)} %copy-done), kind=kOutput, calls=%fused_computation.22 | convolution fusion | flops 301989888 | bytes 1540096 | tf_op jit(solution)/shard_map/dot_general | solution.py:20
  38.3 0.0 reduce-scatter.9.cloned.1.call-start
  38.3 21.1 %reduce-scatter.7.cloned.1.call-done = f32[32,3,256]{2,0,1:T(8,128)} async-done(((f32[32,3,1024]{2,0,1:T(8,128)}), f32[32,3,256]{2,0,1:T(8,128)}) %reduce-scatter.7.cloned.1.call-update) | async-done | bytes 98320 | tf_op jit(solution)/shard_map/reduce_scatter | solution.py:36
  59.4 2.8 %fusion.1 = f32[32,3,1024]{2,0,1:T(8,128)} fusion(f32[2,1024,256]{2,1,0:T(8,128)S(1)} %copy-done.2, f32[32,3,256]{2,0,1:T(8,128)} %reduce-scatter.7.cloned.1.call-done, f32[32,3,1,256]{3,2,1,0:T(1,128)S(1)} %get-tuple-element.9), kind=kOutput, calls=%fused_computation.20 | convolution fusion | flops 302014464 | bytes 1638400 | tf_op jit(solution)/shard_map/dot_general | solution.py:20
  62.2 0.0 reduce-scatter.11.cloned.1.call-start
  62.3 21.1 %reduce-scatter.9.cloned.1.call-done = f32[32,3,256]{2,0,1:T(8,128)} async-done(((f32[32,3,1024]{2,0,1:T(8,128)}), f32[32,3,256]{2,0,1:T(8,128)}) %reduce-scatter.9.cloned.1.call-update) | async-done | bytes 98320 | tf_op jit(solution)/shard_map/reduce_scatter | solution.py:40
  83.3 4.2 %collective-permute-start.3 = (f32[32,3,256]{2,0,1:T(8,128)}, f32[32,3,256]{2,0,1:T(8,128)S(1)}, u32[]{:S(2)}, u32[]{:S(2)}) collective-permute-start(f32[32,3,256]{2,0,1:T(8,128)} %reduce-scatter.9.cloned.1.call-done), channel_id=1, source_target_pairs={{0,28},{4,0},{8,4},{12,8},{16,12},{20,16},{24,20},{28,24},{1,29},{... | collective-permute-start | bytes 294920 | tf_op jit(solution)/shard_map/ppermute | solution.py:12
  87.6 0.6 collective-permute-start
  88.1 2.7 %collective-permute-done.3 = f32[32,3,256]{2,0,1:T(8,128)S(1)} collective-permute-done((f32[32,3,256]{2,0,1:T(8,128)}, f32[32,3,256]{2,0,1:T(8,128)S(1)}, u32[]{:S(2)}, u32[]{:S(2)}) %collective-permute-start.3) | collective-permute-done | bytes 98336 | tf_op jit(solution)/shard_map/ppermute | solution.py:12
  90.8 0.9 pad_maximum_fusion.4
  91.7 1.5 collective-permute-start.4
  93.3 0.8 collective-permute-start.1
  94.0 4.8 %collective-permute-done.4 = f32[64,3,256]{2,0,1:T(8,128)S(1)} collective-permute-done((f32[64,3,256]{2,0,1:T(8,128)S(1)}, f32[64,3,256]{2,0,1:T(8,128)S(1)}, u32[]{:S(2)}, u32[]{:S(2)}) %collective-permute-start.4) | collective-permute-done | bytes 196640 | tf_op jit(solution)/shard_map/ppermute | solution.py:12
  98.8 1.7 pad_maximum_fusion.1
  100.5 0.9 collective-permute-start.5
  101.4 1.4 collective-permute-done.1
  102.8 0.8 pad_maximum_fusion
  103.6 0.7 collective-permute-start.2
  104.3 4.0 %fusion.33 = (f32[1024,1,256]{2,1,0:T(1,128)S(1)}, f32[1024,1,256]{2,1,0:T(1,128)S(1)}) fusion(f32[1024,2,256]{2,1,0:T(2,128)} %param.10), kind=kLoop, calls=%fused_computation.54 | loop fusion | bytes 4194304 | tf_op jit(solution)/shard_map/slice | solution.py:60
  108.4 18.3 %collective-permute-done.5 = f32[128,3,256]{2,0,1:T(8,128)} collective-permute-done((f32[128,3,256]{2,0,1:T(8,128)}, f32[128,3,256]{2,0,1:T(8,128)}, u32[]{:S(2)}, u32[]{:S(2)}) %collective-permute-start.5) | collective-permute-done | bytes 393248 | tf_op jit(solution)/shard_map/ppermute | solution.py:12
  126.7 4.3 %fusion = f32[256,3,1024]{2,0,1:T(8,128)S(1)} fusion(f32[1024,1,256]{2,1,0:T(1,128)S(1)} %get-tuple-element.8, s32[]{:T(128)S(6)} %select_n.13, f32[32,3,256]{2,0,1:T(8,128)S(1)} %copy-done.3, f32[32,3,256]{2,0,1:T(8,128)S(1)} %collective-permute-done.3, f32[64,3,256]{2,0,1:T(8,128)} %copy-done.7, f32[128,3,256]{2,0,1:T(8,128)} %collective-permute-done.5), kind=kOutput, calls=%fused_computation.18 | convolution fusion | flops 2417295360 | bytes 4980740 | tf_op jit(solution)/shard_map/dot_general | solution.py:50
  131.0 3.1 %collective-permute-done.2 = f32[128,3,256]{2,0,1:T(8,128)} collective-permute-done((f32[128,3,256]{2,0,1:T(8,128)}, f32[128,3,256]{2,0,1:T(8,128)}, u32[]{:S(2)}, u32[]{:S(2)}) %collective-permute-start.2) | collective-permute-done | bytes 393248 | tf_op jit(solution)/shard_map/ppermute | solution.py:12
  134.1 5.8 %convolution_add_fusion = f32[256,3,1024]{2,0,1:T(8,128)} fusion(f32[256,3,1024]{2,0,1:T(8,128)S(1)} %fusion, f32[1024,1,256]{2,1,0:T(1,128)S(1)} %get-tuple-element.7, s32[]{:T(128)S(6)} %select_n.13, f32[32,3,256]{2,0,1:T(8,128)S(1)} %copy-done.1, f32[32,3,256]{2,0,1:T(8,128)S(1)} %collective-permute-done, f32[64,3,256]{2,0,1:T(8,128)S(1)} %copy-done.6, ...), kind=kOutput, calls=%fused_computation | convolution fusion | flops 2418081792 | bytes 8126468 | tf_op jit(solution)/shard_map/dot_general | solution.py:50
  139.9 0.8 copy.16
  140.8 40.0 %reduce-scatter.11.cloned.1.call-done = f32[64,3,1024]{2,0,1:T(8,128)} async-done(((f32[256,3,1024]{2,0,1:T(8,128)}), f32[64,3,1024]{2,0,1:T(8,128)}) %reduce-scatter.11.cloned.1.call-update) | async-done | bytes 786448 | tf_op jit(solution)/shard_map/reduce_scatter | solution.py:69
  180.7 2.1 %sub.10 = f32[64,3,1024]{2,0,1:T(8,128)} subtract(f32[64,3,1024]{2,0,1:T(8,128)S(1)} %copy-done.4, f32[64,3,1024]{2,0,1:T(8,128)} %reduce-scatter.11.cloned.1.call-done) | non-fusion elementwise | flops 196608 | bytes 2359296 | tf_op jit(solution)/shard_map/sub | solution.py:72
  (22 shorter events, 0.1 us)
Async XLA Ops:
  7.2 28.3 %copy-start = (f32[1024,256]{1,0:T(8,128)S(1)}, f32[1024,256]{1,0:T(8,128)}, u32[]{:S(2)}) copy-start(f32[1024,256]{1,0:T(8,128)} %param.9) | copy-start | bytes 3145732
  7.2 28.3 %reduce-scatter.5.cloned.1.call-start = ((), (), s32[]{:S(2)}) async-start(), calls=%async_computation.4 | async-start | bytes 491520 | tf_op jit(solution)/shard_map/reduce_scatter | solution.py:30
  8.5 50.9 %copy-start.2 = (f32[2,1024,256]{2,1,0:T(8,128)S(1)}, f32[2,1024,256]{2,1,0:T(8,128)}, u32[]{:S(2)}) copy-start(f32[2,1024,256]{2,1,0:T(8,128)} %param.8) | copy-start | bytes 6291460
  11.8 47.6 %reduce-scatter.7.cloned.1.call-start = ((), (), s32[]{:S(2)}) async-start(), calls=%async_computation.5 | async-start | bytes 491520 | tf_op jit(solution)/shard_map/reduce_scatter | solution.py:36
  38.3 49.3 %copy-start.1 = (f32[32,3,256]{2,0,1:T(8,128)S(1)}, f32[32,3,256]{2,0,1:T(8,128)}, u32[]{:S(2)}) copy-start(f32[32,3,256]{2,0,1:T(8,128)} %reduce-scatter.5.cloned.1.call-done) | copy-start | bytes 294916
  38.3 45.0 %reduce-scatter.9.cloned.1.call-start = ((), (), s32[]{:S(2)}) async-start(), calls=%async_computation.6 | async-start | bytes 491520 | tf_op jit(solution)/shard_map/reduce_scatter | solution.py:40
  62.2 118.5 %reduce-scatter.11.cloned.1.call-start = ((), (), s32[]{:S(2)}) async-start(), calls=%async_computation.7 | async-start | bytes 3932160 | tf_op jit(solution)/shard_map/reduce_scatter | solution.py:69
  83.3 7.5 %collective-permute-start.3 = (f32[32,3,256]{2,0,1:T(8,128)}, f32[32,3,256]{2,0,1:T(8,128)S(1)}, u32[]{:S(2)}, u32[]{:S(2)}) collective-permute-start(f32[32,3,256]{2,0,1:T(8,128)} %reduce-scatter.9.cloned.1.call-done), channel_id=1, source_target_pairs={{0,28},{4,0},{8,4},{12,8},{16,12},{20,16},{24,20},{28,24},{1,29},{... | collective-permute-start | bytes 294920 | tf_op jit(solution)/shard_map/ppermute | solution.py:12
  87.6 5.7 %collective-permute-start = (f32[32,3,256]{2,0,1:T(8,128)S(1)}, f32[32,3,256]{2,0,1:T(8,128)S(1)}, u32[]{:S(2)}, u32[]{:S(2)}) collective-permute-start(f32[32,3,256]{2,0,1:T(8,128)S(1)} %copy-done.1), channel_id=1, source_target_pairs={{0,28},{4,0},{8,4},{12,8},{16,12},{20,16},{24,20},{28,24},{1,29},{... | collective-permute-start | bytes 294920 | tf_op jit(solution)/shard_map/ppermute | solution.py:12
  91.7 7.1 %collective-permute-start.4 = (f32[64,3,256]{2,0,1:T(8,128)S(1)}, f32[64,3,256]{2,0,1:T(8,128)S(1)}, u32[]{:S(2)}, u32[]{:S(2)}) collective-permute-start(f32[64,3,256]{2,0,1:T(8,128)S(1)} %pad_maximum_fusion.4), channel_id=1, source_target_pairs={{0,24},{4,28},{8,0},{12,4},{16,8},{20,12},{24,16},{28,20},{1,25},{... | collective-permute-start | bytes 589832 | tf_op jit(solution)/shard_map/ppermute | solution.py:12
  93.3 9.5 %collective-permute-start.1 = (f32[64,3,256]{2,0,1:T(8,128)S(1)}, f32[64,3,256]{2,0,1:T(8,128)S(1)}, u32[]{:S(2)}, u32[]{:S(2)}) collective-permute-start(f32[64,3,256]{2,0,1:T(8,128)S(1)} %pad_maximum_fusion.3), channel_id=1, source_target_pairs={{0,24},{4,28},{8,0},{12,4},{16,8},{20,12},{24,16},{28,20},{1,25},{... | collective-permute-start | bytes 589832 | tf_op jit(solution)/shard_map/ppermute | solution.py:12
  98.8 4.8 %copy-start.7 = (f32[64,3,256]{2,0,1:T(8,128)}, f32[64,3,256]{2,0,1:T(8,128)S(1)}, u32[]{:S(2)}) copy-start(f32[64,3,256]{2,0,1:T(8,128)S(1)} %collective-permute-done.4) | copy-start | bytes 589828
  100.5 26.1 %collective-permute-start.5 = (f32[128,3,256]{2,0,1:T(8,128)}, f32[128,3,256]{2,0,1:T(8,128)}, u32[]{:S(2)}, u32[]{:S(2)}) collective-permute-start(f32[128,3,256]{2,0,1:T(8,128)} %pad_maximum_fusion.1), channel_id=1, source_target_pairs={{0,16},{4,20},{8,24},{12,28},{16,0},{20,4},{24,8},{28,12},{1,17},{... | collective-permute-start | bytes 1179656 | tf_op jit(solution)/shard_map/ppermute | solution.py:12
  102.8 0.8 copy-start.5
  103.6 23.1 %copy-start.3 = (f32[32,3,256]{2,0,1:T(8,128)S(1)}, f32[32,3,256]{2,0,1:T(8,128)}, u32[]{:S(2)}) copy-start(f32[32,3,256]{2,0,1:T(8,128)} %reduce-scatter.9.cloned.1.call-done) | copy-start | bytes 294916
  103.6 30.4 %collective-permute-start.2 = (f32[128,3,256]{2,0,1:T(8,128)}, f32[128,3,256]{2,0,1:T(8,128)}, u32[]{:S(2)}, u32[]{:S(2)}) collective-permute-start(f32[128,3,256]{2,0,1:T(8,128)} %pad_maximum_fusion), channel_id=1, source_target_pairs={{0,16},{4,20},{8,24},{12,28},{16,0},{20,4},{24,8},{28,12},{1,17},{... | collective-permute-start | bytes 1179656 | tf_op jit(solution)/shard_map/ppermute | solution.py:12
  126.7 7.4 %copy-start.6 = (f32[64,3,256]{2,0,1:T(8,128)S(1)}, f32[64,3,256]{2,0,1:T(8,128)}, u32[]{:S(2)}) copy-start(f32[64,3,256]{2,0,1:T(8,128)} %copy-done.5) | copy-start | bytes 589828
  139.9 40.8 %copy-start.4 = (f32[64,3,1024]{2,0,1:T(8,128)S(1)}, f32[64,3,1024]{2,0,1:T(8,128)}, u32[]{:S(2)}) copy-start(f32[64,3,1024]{2,0,1:T(8,128)} %param.11) | copy-start | bytes 2359300
Sparse Core Ops, SparseCore 0:
  11.9 23.5 reduce-scatter.4
  38.6 20.8 reduce-scatter.6
  62.5 20.8 reduce-scatter.8
  140.0 40.6 reduce-scatter.10
